TPU v7x, 32 devices: a whole 2x2x4 slice. The times are simulated.
32 devices in a mesh: groups: 2 (over x), ctx: 16 (over z, y, core).
Axes of the slice: x: 2, y: 2, z: 4, core: 2. Of those that a mesh axis runs over, the one named last changes fastest.
Arguments:
- queries: bfloat16 [16384, 3584], P(('groups', 'ctx')), parts along dimension 0, may hold values from -48 to 48
- keys: bfloat16 [16384, 512], P(('groups', 'ctx')), parts along dimension 0, may hold values from -6 to 6
- values: bfloat16 [16384, 512], P(('groups', 'ctx')), parts along dimension 0, may hold values from -6 to 6
- out_grad: bfloat16 [16384, 3584], P(('groups', 'ctx')), parts along dimension 0, may hold values from -6 to 6
- links: int32 [128, 4], P(('groups', 'ctx')), parts along dimension 0, may hold values from -1 to 3, as said below
- header_blocks: int32 [8], P('groups'), parts along dimension 0, may hold values from 0 to 59, as said below
Outputs:
- query_grad: bfloat16 [16384, 3584], P(('groups', 'ctx')), parts along dimension 0
- key_gradient_array: float32 [16384, 512], P(('groups', 'ctx')), parts along dimension 0
- value_gradient_array: float32 [16384, 512], P(('groups', 'ctx')), parts along dimension 0
There are 2 independent parts, one for each index of `groups`. A program takes and returns all parts, laid end to end along the dimension named above; each array names one. Nothing has to cross between parts.
Inputs may be any that keep to these rules, and one draw needn't show every extreme that they name: `header_blocks`: strictly increasing; no two header blocks lie among the same aligned 4 blocks, and none lies among the last 4 blocks. Non-empty entries of one row are distinct header numbers whose header block ends before the row's window part begins (header_blocks[links[b, l]] <= b - 256 / 128 - 1). The last row has no empty entry.
All inputs are finite; a program needn't handle non-finite values.
Results may differ from a plain program's by a relative error of at most 0.012.
Values may be sent and summed in bfloat16 or wider, within the bound.
A program may use at most 192 MiB of HBM per device.

v0:
```python
import jax
import jax.numpy as jnp
from jax import lax
from jax.sharding import PartitionSpec as P

QUERY_HEADS = 28
KEY_VALUE_HEADS = 4
HEAD_SIZE = 128
BLK = 128
WIN = 256
LINKS = 4


def shifted(x, axis, by):
    peers = lax.axis_size(axis)
    pairs = [(i, i + by) for i in range(peers) if 0 <= i + by < peers]
    return lax.ppermute(x, axis, pairs)


def block_grads(query_row_block, gradient_row_block, key_row_block, value_row_block, is_valid):
    row_total_count = query_row_block.shape[0]
    key_total_count = key_row_block.shape[0]
    queries_each_group = QUERY_HEADS // KEY_VALUE_HEADS
    factor = float(HEAD_SIZE) ** (-0.5)
    query_four_axes = query_row_block.reshape(
        row_total_count, KEY_VALUE_HEADS, queries_each_group, HEAD_SIZE
    )
    gradient_four_axes = gradient_row_block.reshape(
        row_total_count, KEY_VALUE_HEADS, queries_each_group, HEAD_SIZE
    )
    key_three_axes = key_row_block.reshape(key_total_count, KEY_VALUE_HEADS, HEAD_SIZE)
    value_three_axes = value_row_block.reshape(key_total_count, KEY_VALUE_HEADS, HEAD_SIZE)
    scores = (
        jnp.einsum(
            "qgrd,kgd->gqrk", query_four_axes, key_three_axes, preferred_element_type=jnp.float32
        )
        * factor
    )
    scores = jnp.where(is_valid[None, :, None, :], scores, -1e30)
    row_max = jnp.max(scores, axis=-1, keepdims=True)
    weights = jnp.exp(scores - row_max)
    attend = weights / jnp.sum(weights, axis=-1, keepdims=True)
    d_attend = jnp.einsum(
        "qgrd,kgd->gqrk", gradient_four_axes, value_three_axes, preferred_element_type=jnp.float32
    )
    row_delta = jnp.sum(attend * d_attend, axis=-1, keepdims=True)
    d_scores = (attend * (d_attend - row_delta) * factor).astype(jnp.bfloat16)
    attend_low = attend.astype(jnp.bfloat16)
    query_grad = jnp.einsum(
        "gqrk,kgd->qgrd", d_scores, key_three_axes, preferred_element_type=jnp.float32
    )
    key_gradient_array = jnp.einsum(
        "gqrk,qgrd->kgd", d_scores, query_four_axes, preferred_element_type=jnp.float32
    )
    value_gradient_array = jnp.einsum(
        "gqrk,qgrd->kgd", attend_low, gradient_four_axes, preferred_element_type=jnp.float32
    )
    key_value_gradient = jnp.concatenate(
        [
            key_gradient_array.reshape(key_total_count, KEY_VALUE_HEADS * HEAD_SIZE),
            value_gradient_array.reshape(key_total_count, KEY_VALUE_HEADS * HEAD_SIZE),
        ],
        axis=1,
    )
    return (query_grad.reshape(row_total_count, QUERY_HEADS * HEAD_SIZE), key_value_gradient)


def body(queries, keys, values, out_grad, links, header_blocks):
    row_total_count = queries.shape[0]
    block_count = row_total_count // BLK
    half_width = keys.shape[1]
    my_index = lax.axis_index("ctx")
    kv_local = jnp.concatenate([keys, values], axis=1)
    kv_width = kv_local.shape[1]
    previous = shifted(kv_local[row_total_count - WIN :], "ctx", 1)
    extended = jnp.concatenate([previous, kv_local], axis=0)
    owners = header_blocks // block_count
    offsets = header_blocks % block_count
    is_mine = owners == my_index
    pick_table = (
        is_mine[:, None] & (offsets[:, None] == jnp.arange(block_count, dtype=jnp.int32)[None, :])
    ).astype(jnp.float32)
    select = jnp.sum(pick_table, axis=0)
    kv_blocks = kv_local.reshape(block_count, BLK * kv_width)
    own_slot = jnp.dot(
        select[None, :].astype(jnp.bfloat16), kv_blocks, preferred_element_type=jnp.float32
    ).astype(jnp.bfloat16)
    header_table = lax.all_gather(own_slot.reshape(1, BLK, kv_width), "ctx", axis=0, tiled=True)
    holders = header_table.shape[0]
    window_span = WIN + BLK

    def one_block(carry, block_id):
        near_acc, far_acc = carry
        row_start = block_id * BLK
        query_row_block = lax.dynamic_slice_in_dim(queries, row_start, BLK, 0)
        gradient_row_block = lax.dynamic_slice_in_dim(out_grad, row_start, BLK, 0)
        window = lax.dynamic_slice_in_dim(extended, row_start, window_span, 0)
        entries = links[block_id]
        is_live = entries >= 0
        safe_slot = jnp.where(is_live, entries, 0)
        holder = owners[safe_slot]
        fetched = header_table[holder].reshape(LINKS * BLK, kv_width)
        key_tile = jnp.concatenate([window, fetched], axis=0)
        q_pos = my_index * row_total_count + row_start + jnp.arange(BLK, dtype=jnp.int32)
        k_pos = (
            my_index * row_total_count + row_start - WIN + jnp.arange(window_span, dtype=jnp.int32)
        )
        near_ok = (
            (k_pos[None, :] <= q_pos[:, None])
            & (q_pos[:, None] - k_pos[None, :] < WIN)
            & (k_pos[None, :] >= 0)
        )
        far_ok = jnp.broadcast_to(jnp.repeat(is_live, BLK)[None, :], (BLK, LINKS * BLK))
        is_valid = jnp.concatenate([near_ok, far_ok], axis=1)
        query_grad, key_value_gradient = block_grads(
            query_row_block,
            gradient_row_block,
            key_tile[:, :half_width],
            key_tile[:, half_width:],
            is_valid,
        )
        current = lax.dynamic_slice_in_dim(near_acc, row_start, window_span, 0)
        near_acc = lax.dynamic_update_slice_in_dim(
            near_acc, current + key_value_gradient[:window_span], row_start, 0
        )
        far_grad = (
            key_value_gradient[window_span:].reshape(LINKS, BLK, kv_width)
            * is_live.astype(jnp.float32)[:, None, None]
        )
        far_acc = far_acc.at[holder].add(far_grad)
        return ((near_acc, far_acc), query_grad.astype(jnp.bfloat16))

    start_near = jnp.zeros((WIN + row_total_count, kv_width), jnp.float32)
    start_far = jnp.zeros((holders, BLK, kv_width), jnp.float32)
    (near_acc, far_acc), dq_blocks = lax.scan(
        one_block, (start_near, start_far), jnp.arange(block_count, dtype=jnp.int32)
    )
    query_out = dq_blocks.reshape(row_total_count, QUERY_HEADS * HEAD_SIZE)
    returned = shifted(near_acc[:WIN], "ctx", -1)
    local_grad = near_acc[WIN:]
    local_grad = local_grad.at[row_total_count - WIN :].add(returned)
    own_grad = lax.psum_scatter(far_acc, "ctx", scatter_dimension=0, tiled=True)
    own_part = select[:, None] * own_grad.reshape(1, BLK * kv_width)
    local_grad = local_grad + own_part.reshape(row_total_count, kv_width)
    return (query_out, local_grad[:, :half_width], local_grad[:, half_width:])


def solution(mesh):
    in_specs = (
        P(("groups", "ctx"), None),
        P(("groups", "ctx"), None),
        P(("groups", "ctx"), None),
        P(("groups", "ctx"), None),
        P(("groups", "ctx"), None),
        P("groups"),
    )
    out_specs = (P(("groups", "ctx"), None), P(("groups", "ctx"), None), P(("groups", "ctx"), None))
    return jax.shard_map(body, mesh=mesh, in_specs=in_specs, out_specs=out_specs, check_vma=False)
```

profile of v0, /device:TPU:0, one launch (start us, length us, event | category | flops | bytes accessed | tf_op | source)
XLA Modules:
  0.0 728.5 jit_solution(8349914909638249145)
XLA Ops:
  19.4 48.0 %all-gather.2.cloned.1.call-done = bf16[16,128,1024]{2,1,0:T(8,128)(2,1)} async-done(((bf16[1,128,1024]{2,1,0:T(8,128)(2,1)}), bf16[16,128,1024]{2,1,0:T(8,128)(2,1)}) %all-gather.2.cloned.1.call-update) | async-done | bytes 4194320 | tf_op jit(solution)/shard_map/all_gather | solution.py:88
  69.4 4.3 broadcast_in_dim.69
  73.7 542.4 %while.17 = (s32[]{:T(128)}, f32[768,1024]{1,0:T(8,128)}, f32[16,128,1024]{2,1,0:T(8,128)}, bf16[4,128,3584]{2,1,0:T(8,128)(2,1)}, s32[4]{0:T(128)S(1)}, /*index...) while((s32[]{:T(128)}, f32[768,1024]{1,0:T(8,128)}, ...), condition=%wide.region_6.7_spmd, body=%wide.region_1.6_spmd.sunk | while | flops 4181505024 | bytes 192610576 | solution.py:135
  92.6 6.5 fusion.86
  99.1 11.3 %fusion.84 = (f32[4,128,7]{1,2,0:T(8,128)}, f32[4,128,7,896]{3,1,2,0:T(8,128)}) fusion(pred[128,896]{1,0:T(8,128)(4,1)S(1)} %pad_add_fusion.2, bf16[128,4,7,128]{0,3,2,1:T(8,128)(2,1)} %bitcast.124, bf16[896,4,128,1]{0,2,3,1:T(8,128)(2,1)} %bitcast.121), kind=kOutput, calls=%fused_computation.78.clone.1 | convolution fusion | flops 834929536 | bytes 14809088 | tf_op jit(solution)/shard_map/while/body/eval_jaxpr/sub | solution.py:41
  110.4 36.7 %fusion.88 = bf16[4,128,128,7]{2,1,3,0:T(8,128)(2,1)} fusion(bf16[896,4,128,1]{0,2,3,1:T(8,128)(2,1)S(1)} %bitcast.122, f32[4,128,7,896]{3,1,2,0:T(8,128)} %fusion.86, f32[4,128,7,896]{3,1,2,0:T(8,128)} %get-tuple-element.340, f32[4,128,7]{1,2,0:T(8,128)} %get-tuple-element.341), kind=kOutput, calls=%fused_computation.23.clone.1 | convolution fusion | flops 845025664 | bytes 27539456 | tf_op jit(solution)/shard_map/while/body/eval_jaxpr/gqrk,kgd->qgrd/dot_general | solution.py:49
  147.1 36.2 %fusion.87 = f32[4,128,896,1]{2,1,3,0:T(8,128)S(1)} fusion(bf16[128,4,7,128]{0,3,2,1:T(8,128)(2,1)} %bitcast.125, f32[4,128,7,896]{3,1,2,0:T(8,128)} %fusion.86, f32[4,128,7,896]{3,1,2,0:T(8,128)} %get-tuple-element.340, f32[4,128,7]{1,2,0:T(8,128)S(1)} %copy-done.9), kind=kOutput, calls=%fused_computation.18.clone.1 | convolution fusion | flops 844566912 | bytes 28456960 | tf_op jit(solution)/shard_map/while/body/eval_jaxpr/gqrk,qgrd->kgd/dot_general | solution.py:52
  183.4 7.0 fusion.85
  228.2 6.5 fusion.86
  234.7 11.3 %fusion.84 = (f32[4,128,7]{1,2,0:T(8,128)}, f32[4,128,7,896]{3,1,2,0:T(8,128)}) fusion(pred[128,896]{1,0:T(8,128)(4,1)S(1)} %pad_add_fusion.2, bf16[128,4,7,128]{0,3,2,1:T(8,128)(2,1)} %bitcast.124, bf16[896,4,128,1]{0,2,3,1:T(8,128)(2,1)} %bitcast.121), kind=kOutput, calls=%fused_computation.78.clone.1 | convolution fusion | flops 834929536 | bytes 14809088 | tf_op jit(solution)/shard_map/while/body/eval_jaxpr/sub | solution.py:41
  246.0 36.7 %fusion.88 = bf16[4,128,128,7]{2,1,3,0:T(8,128)(2,1)} fusion(bf16[896,4,128,1]{0,2,3,1:T(8,128)(2,1)S(1)} %bitcast.122, f32[4,128,7,896]{3,1,2,0:T(8,128)} %fusion.86, f32[4,128,7,896]{3,1,2,0:T(8,128)} %get-tuple-element.340, f32[4,128,7]{1,2,0:T(8,128)} %get-tuple-element.341), kind=kOutput, calls=%fused_computation.23.clone.1 | convolution fusion | flops 845025664 | bytes 27539456 | tf_op jit(solution)/shard_map/while/body/eval_jaxpr/gqrk,kgd->qgrd/dot_general | solution.py:49
  282.7 36.2 %fusion.87 = f32[4,128,896,1]{2,1,3,0:T(8,128)S(1)} fusion(bf16[128,4,7,128]{0,3,2,1:T(8,128)(2,1)} %bitcast.125, f32[4,128,7,896]{3,1,2,0:T(8,128)} %fusion.86, f32[4,128,7,896]{3,1,2,0:T(8,128)} %get-tuple-element.340, f32[4,128,7]{1,2,0:T(8,128)S(1)} %copy-done.9), kind=kOutput, calls=%fused_computation.18.clone.1 | convolution fusion | flops 844566912 | bytes 28456960 | tf_op jit(solution)/shard_map/while/body/eval_jaxpr/gqrk,qgrd->kgd/dot_general | solution.py:52
  319.0 7.0 fusion.85
  363.8 6.5 fusion.86
  370.3 11.3 %fusion.84 = (f32[4,128,7]{1,2,0:T(8,128)}, f32[4,128,7,896]{3,1,2,0:T(8,128)}) fusion(pred[128,896]{1,0:T(8,128)(4,1)S(1)} %pad_add_fusion.2, bf16[128,4,7,128]{0,3,2,1:T(8,128)(2,1)} %bitcast.124, bf16[896,4,128,1]{0,2,3,1:T(8,128)(2,1)} %bitcast.121), kind=kOutput, calls=%fused_computation.78.clone.1 | convolution fusion | flops 834929536 | bytes 14809088 | tf_op jit(solution)/shard_map/while/body/eval_jaxpr/sub | solution.py:41
  381.6 36.7 %fusion.88 = bf16[4,128,128,7]{2,1,3,0:T(8,128)(2,1)} fusion(bf16[896,4,128,1]{0,2,3,1:T(8,128)(2,1)S(1)} %bitcast.122, f32[4,128,7,896]{3,1,2,0:T(8,128)} %fusion.86, f32[4,128,7,896]{3,1,2,0:T(8,128)} %get-tuple-element.340, f32[4,128,7]{1,2,0:T(8,128)} %get-tuple-element.341), kind=kOutput, calls=%fused_computation.23.clone.1 | convolution fusion | flops 845025664 | bytes 27539456 | tf_op jit(solution)/shard_map/while/body/eval_jaxpr/gqrk,kgd->qgrd/dot_general | solution.py:49
  418.4 36.2 %fusion.87 = f32[4,128,896,1]{2,1,3,0:T(8,128)S(1)} fusion(bf16[128,4,7,128]{0,3,2,1:T(8,128)(2,1)} %bitcast.125, f32[4,128,7,896]{3,1,2,0:T(8,128)} %fusion.86, f32[4,128,7,896]{3,1,2,0:T(8,128)} %get-tuple-element.340, f32[4,128,7]{1,2,0:T(8,128)S(1)} %copy-done.9), kind=kOutput, calls=%fused_computation.18.clone.1 | convolution fusion | flops 844566912 | bytes 28456960 | tf_op jit(solution)/shard_map/while/body/eval_jaxpr/gqrk,qgrd->kgd/dot_general | solution.py:52
  454.6 7.0 fusion.85
  499.5 6.5 fusion.86
  505.9 11.3 %fusion.84 = (f32[4,128,7]{1,2,0:T(8,128)}, f32[4,128,7,896]{3,1,2,0:T(8,128)}) fusion(pred[128,896]{1,0:T(8,128)(4,1)S(1)} %pad_add_fusion.2, bf16[128,4,7,128]{0,3,2,1:T(8,128)(2,1)} %bitcast.124, bf16[896,4,128,1]{0,2,3,1:T(8,128)(2,1)} %bitcast.121), kind=kOutput, calls=%fused_computation.78.clone.1 | convolution fusion | flops 834929536 | bytes 14809088 | tf_op jit(solution)/shard_map/while/body/eval_jaxpr/sub | solution.py:41
  517.3 36.7 %fusion.88 = bf16[4,128,128,7]{2,1,3,0:T(8,128)(2,1)} fusion(bf16[896,4,128,1]{0,2,3,1:T(8,128)(2,1)S(1)} %bitcast.122, f32[4,128,7,896]{3,1,2,0:T(8,128)} %fusion.86, f32[4,128,7,896]{3,1,2,0:T(8,128)} %get-tuple-element.340, f32[4,128,7]{1,2,0:T(8,128)} %get-tuple-element.341), kind=kOutput, calls=%fused_computation.23.clone.1 | convolution fusion | flops 845025664 | bytes 27539456 | tf_op jit(solution)/shard_map/while/body/eval_jaxpr/gqrk,kgd->qgrd/dot_general | solution.py:49
  554.0 36.2 %fusion.87 = f32[4,128,896,1]{2,1,3,0:T(8,128)S(1)} fusion(bf16[128,4,7,128]{0,3,2,1:T(8,128)(2,1)} %bitcast.125, f32[4,128,7,896]{3,1,2,0:T(8,128)} %fusion.86, f32[4,128,7,896]{3,1,2,0:T(8,128)} %get-tuple-element.340, f32[4,128,7]{1,2,0:T(8,128)S(1)} %copy-done.9), kind=kOutput, calls=%fused_computation.18.clone.1 | convolution fusion | flops 844566912 | bytes 28456960 | tf_op jit(solution)/shard_map/while/body/eval_jaxpr/gqrk,qgrd->kgd/dot_general | solution.py:52
  590.2 7.0 fusion.85
  624.3 94.0 %reduce-scatter.2.cloned.1.call-done = f32[1,128,1024]{2,1,0:T(8,128)} async-done(((f32[16,128,1024]{2,1,0:T(8,128)}), f32[1,128,1024]{2,1,0:T(8,128)}) %reduce-scatter.2.cloned.1.call-update) | async-done | bytes 524304 | tf_op jit(solution)/shard_map/reduce_scatter | solution.py:142
  (214 shorter events, 166.1 us)
Async XLA Ops:
  7.2 60.2 %all-gather.2.cloned.1.call-start = ((), (), s32[]{:S(2)}) async-start(), calls=%async_computation.1 | async-start | bytes 4456448 | tf_op jit(solution)/shard_map/all_gather | solution.py:88
  14.1 704.1 %reduce-scatter.2.cloned.1.call-start = ((), (), s32[]{:S(2)}) async-start(), calls=%async_computation.2 | async-start | bytes 8912896 | tf_op jit(solution)/shard_map/reduce_scatter | solution.py:142
  14.2 3.9 collective-permute-start
  85.6 7.0 copy-start.1
  90.0 9.1 %copy-start.2 = (bf16[128,3584]{0,1:T(8,128)(2,1)}, bf16[128,3584]{0,1:T(8,128)(2,1)S(1)}, u32[]{:S(2)}) copy-start(bf16[128,3584]{0,1:T(8,128)(2,1)S(1)} %copy.104) | copy-start | bytes 2752516 | tf_op jit(solution)/shard_map/while
  99.1 11.3 %copy-start.5 = (bf16[896,512]{0,1:T(8,128)(2,1)S(1)}, bf16[896,512]{0,1:T(8,128)(2,1)}, u32[]{:S(2)}) copy-start(bf16[896,512]{0,1:T(8,128)(2,1)} %get-tuple-element.339) | copy-start | bytes 2752516 | tf_op jit(solution)/shard_map/while
  110.4 36.7 %copy-start.9 = (f32[4,128,7]{1,2,0:T(8,128)S(1)}, f32[4,128,7]{1,2,0:T(8,128)}, u32[]{:S(2)}) copy-start(f32[4,128,7]{1,2,0:T(8,128)} %get-tuple-element.341) | copy-start | bytes 43012 | tf_op jit(solution)/shard_map/while
  183.4 7.0 copy-start
  221.2 7.0 copy-start.1
  225.7 9.1 %copy-start.2 = (bf16[128,3584]{0,1:T(8,128)(2,1)}, bf16[128,3584]{0,1:T(8,128)(2,1)S(1)}, u32[]{:S(2)}) copy-start(bf16[128,3584]{0,1:T(8,128)(2,1)S(1)} %copy.104) | copy-start | bytes 2752516 | tf_op jit(solution)/shard_map/while
  234.7 11.3 %copy-start.5 = (bf16[896,512]{0,1:T(8,128)(2,1)S(1)}, bf16[896,512]{0,1:T(8,128)(2,1)}, u32[]{:S(2)}) copy-start(bf16[896,512]{0,1:T(8,128)(2,1)} %get-tuple-element.339) | copy-start | bytes 2752516 | tf_op jit(solution)/shard_map/while
  246.0 36.7 %copy-start.9 = (f32[4,128,7]{1,2,0:T(8,128)S(1)}, f32[4,128,7]{1,2,0:T(8,128)}, u32[]{:S(2)}) copy-start(f32[4,128,7]{1,2,0:T(8,128)} %get-tuple-element.341) | copy-start | bytes 43012 | tf_op jit(solution)/shard_map/while
  319.0 7.0 copy-start
  356.8 7.0 copy-start.1
  361.3 9.1 %copy-start.2 = (bf16[128,3584]{0,1:T(8,128)(2,1)}, bf16[128,3584]{0,1:T(8,128)(2,1)S(1)}, u32[]{:S(2)}) copy-start(bf16[128,3584]{0,1:T(8,128)(2,1)S(1)} %copy.104) | copy-start | bytes 2752516 | tf_op jit(solution)/shard_map/while
  370.3 11.3 %copy-start.5 = (bf16[896,512]{0,1:T(8,128)(2,1)S(1)}, bf16[896,512]{0,1:T(8,128)(2,1)}, u32[]{:S(2)}) copy-start(bf16[896,512]{0,1:T(8,128)(2,1)} %get-tuple-element.339) | copy-start | bytes 2752516 | tf_op jit(solution)/shard_map/while
  381.6 36.7 %copy-start.9 = (f32[4,128,7]{1,2,0:T(8,128)S(1)}, f32[4,128,7]{1,2,0:T(8,128)}, u32[]{:S(2)}) copy-start(f32[4,128,7]{1,2,0:T(8,128)} %get-tuple-element.341) | copy-start | bytes 43012 | tf_op jit(solution)/shard_map/while
  454.6 7.0 copy-start
  492.4 7.0 copy-start.1
  496.9 9.1 %copy-start.2 = (bf16[128,3584]{0,1:T(8,128)(2,1)}, bf16[128,3584]{0,1:T(8,128)(2,1)S(1)}, u32[]{:S(2)}) copy-start(bf16[128,3584]{0,1:T(8,128)(2,1)S(1)} %copy.104) | copy-start | bytes 2752516 | tf_op jit(solution)/shard_map/while
  505.9 11.3 %copy-start.5 = (bf16[896,512]{0,1:T(8,128)(2,1)S(1)}, bf16[896,512]{0,1:T(8,128)(2,1)}, u32[]{:S(2)}) copy-start(bf16[896,512]{0,1:T(8,128)(2,1)} %get-tuple-element.339) | copy-start | bytes 2752516 | tf_op jit(solution)/shard_map/while
  517.3 36.7 %copy-start.9 = (f32[4,128,7]{1,2,0:T(8,128)S(1)}, f32[4,128,7]{1,2,0:T(8,128)}, u32[]{:S(2)}) copy-start(f32[4,128,7]{1,2,0:T(8,128)} %get-tuple-element.341) | copy-start | bytes 43012 | tf_op jit(solution)/shard_map/while
  590.2 7.0 copy-start
  618.1 5.0 collective-permute-start.1
  (8 other events, 20.4 us)
Sparse Core Ops, SparseCore 0:
  14.3 53.0 all-gather.1
  616.3 101.9 reduce-scatter.1
where the time goes:
time: 731 us; the launch traced here: 729 us
  matrix products  392 us (54%)
  waiting for transfers between devices  146 us (20%)
  local copies, waits for them, and re-layouts  115 us (16%)
  other arithmetic  47.7 us (7%)
  between operations  14.2 us (2%)
  loops' own time  11.1 us (2%)
    dot_general x4, matrix products, block_grads(): jnp.einsum('gqrk,kgd->qgrd', d_scores, key_three_axes, preferred_element_...  147 us
    dot_general x4, matrix products, block_grads(): jnp.einsum('gqrk,qgrd->kgd', d_scores, query_four_axes, preferred_element...  145 us
    reduce_scatter x1, waiting for transfers between devices, body(): own_grad = lax.psum_scatter(far_acc, 'ctx', scatter_dimension=0, tiled=True)  94 us
    all_gather x1, waiting for transfers between devices, body(): lax.all_gather(own_slot.reshape(1, BLK, kv_width), 'ctx', axis=0, tiled=T...  48 us
    sub x4, matrix products, block_grads(): weights = jnp.exp(scores - row_max)  45.2 us
    dot_general x4, matrix products, block_grads(): jnp.einsum('gqrk,qgrd->kgd', attend_low, gradient_four_axes, preferred_el...  28.1 us
    dot_general x4, matrix products, block_grads(): jnp.einsum('qgrd,kgd->gqrk', gradient_four_axes, value_three_axes, prefer...  25.9 us
    dynamic_update_slice x8, local copies, waits for them, and re-layouts, one_block(): lax.dynamic_update_slice_in_dim(near_acc, current + key_value_gradient[:w...  23.1 us
  transfers between devices with their start and end apart: 4, of which 4 were waited for; matrix products, arithmetic and copies ran while one was open for 1% of the time, Pallas kernels for 0%

commit v1 on v0

v1 whole, which is shorter than its diff:
```python
import functools
import math

import jax
import jax.numpy as jnp
from jax import lax
from jax.experimental import pallas as pl
from jax.experimental.pallas import tpu as pltpu
from jax.sharding import PartitionSpec as P

QUERY_HEADS = 28
KEY_VALUE_HEADS = 4
HEAD_SIZE = 128
BLK = 128
WIN = 256
LINKS = 4
REP = QUERY_HEADS // KEY_VALUE_HEADS
CHUNKS = 2
FACTOR = float(HEAD_SIZE) ** (-0.5)
EXP2_FACTOR = FACTOR * math.log2(math.e)
NT = (((1,), (1,)), ((), ()))


def shifted(x, axis, by):
    peers = lax.axis_size(axis)
    pairs = [(i, i + by) for i in range(peers) if 0 <= i + by < peers]
    return lax.ppermute(x, axis, pairs)


def dot(a, b, dims=(((1,), (0,)), ((), ()))):
    return lax.dot_general(a, b, dims, preferred_element_type=jnp.float32)


def grad_kernel(block_count, links, headers, index, q_ref, o_ref, k_ref, v_ref, hk_ref, hv_ref, prev_ref,
                dq_ref, near_ref, far_ref, kcat, vcat, ds_s, p_s, near_acc, far_acc):
    b = pl.program_id(1)
    first = index[0] * block_count + b
    row = pl.multiple_of(b * BLK, BLK)

    @pl.when(b == 0)
    def _():
        near_acc[...] = jnp.zeros_like(near_acc)
        far_acc[...] = jnp.zeros_like(far_acc)

    kcat[0:3 * BLK] = k_ref[pl.ds(row, 3 * BLK), :]
    vcat[0:3 * BLK] = v_ref[pl.ds(row, 3 * BLK), :]
    live = jnp.int32(0)
    slots = [jnp.int32(0)] * LINKS
    for l in range(LINKS):
        entry = links[b, l]
        holder = headers[jnp.maximum(entry, 0)] // block_count
        for s in range(l + 1):
            slots[s] = jnp.where((entry >= 0) & (live == s), holder, slots[s])
        live = live + jnp.where(entry >= 0, 1, 0).astype(jnp.int32)
    slots = [pl.multiple_of(s * BLK, BLK) for s in slots]

    key_at = lax.broadcasted_iota(jnp.int32, (BLK, BLK), 0)
    query_at = lax.broadcasted_iota(jnp.int32, (BLK, BLK), 1)
    current = key_at <= query_at
    bias0 = jnp.where(first >= 2, 0.0, -1e30).astype(jnp.float32)
    bias1 = jnp.where(first >= 1, 0.0, -1e30).astype(jnp.float32)

    def work(n):
        for s in range(n):
            kcat[(3 + s) * BLK:(4 + s) * BLK] = hk_ref[pl.ds(slots[s], BLK), :]
            vcat[(3 + s) * BLK:(4 + s) * BLK] = hv_ref[pl.ds(slots[s], BLK), :]
        total = (3 + n) * BLK
        for h in range(REP):
            cols = slice(h * HEAD_SIZE, (h + 1) * HEAD_SIZE)
            st = dot(kcat[0:total], q_ref[:, cols], NT)
            dpt = dot(vcat[0:total], o_ref[:, cols], NT)
            x = [jnp.where(current, st[2 * BLK:3 * BLK], st[0:BLK] + bias0), st[BLK:2 * BLK] + bias1]
            d = [jnp.where(current, dpt[2 * BLK:3 * BLK], dpt[0:BLK]), dpt[BLK:2 * BLK]]
            for s in range(n):
                x.append(st[(3 + s) * BLK:(4 + s) * BLK])
                d.append(dpt[(3 + s) * BLK:(4 + s) * BLK])
            top = x[0]
            for t in x[1:]:
                top = jnp.maximum(top, t)
            top = jnp.max(top, axis=0, keepdims=True)
            e = [jnp.exp2((t - top) * EXP2_FACTOR) for t in x]
            norm = e[0]
            mixed = e[0] * d[0]
            for et, dt in zip(e[1:], d[1:]):
                norm = norm + et
                mixed = mixed + et * dt
            inverse = 1.0 / jnp.sum(norm, axis=0, keepdims=True)
            delta = jnp.sum(mixed, axis=0, keepdims=True) * inverse
            for t, (et, dt) in enumerate(zip(e, d)):
                p = et * inverse
                ds = p * (dt - delta)
                if t == 0:
                    p_s[2 * BLK:3 * BLK, cols] = jnp.where(current, p, 0.0).astype(jnp.bfloat16)
                    p_s[0:BLK, cols] = jnp.where(current, 0.0, p).astype(jnp.bfloat16)
                    ds_s[2 * BLK:3 * BLK, cols] = jnp.where(current, ds, 0.0).astype(jnp.bfloat16)
                    ds_s[0:BLK, cols] = jnp.where(current, 0.0, ds).astype(jnp.bfloat16)
                else:
                    place = BLK if t == 1 else (t + 1) * BLK
                    p_s[place:place + BLK, cols] = p.astype(jnp.bfloat16)
                    ds_s[place:place + BLK, cols] = ds.astype(jnp.bfloat16)
        q_rows = jnp.concatenate([q_ref[:, h * HEAD_SIZE:(h + 1) * HEAD_SIZE] for h in range(REP)], axis=0)
        dk = dot(ds_s[0:total], q_rows) * FACTOR
        o_rows = jnp.concatenate([o_ref[:, h * HEAD_SIZE:(h + 1) * HEAD_SIZE] for h in range(REP)], axis=0)
        dv = dot(p_s[0:total], o_rows)
        near_acc[pl.ds(row, 3 * BLK), 0:HEAD_SIZE] += dk[0:3 * BLK]
        near_acc[pl.ds(row, 3 * BLK), HEAD_SIZE:] += dv[0:3 * BLK]
        for s in range(n):
            far_acc[pl.ds(slots[s], BLK), 0:HEAD_SIZE] += dk[(3 + s) * BLK:(4 + s) * BLK]
            far_acc[pl.ds(slots[s], BLK), HEAD_SIZE:] += dv[(3 + s) * BLK:(4 + s) * BLK]
        dqt = dot(kcat[0:total].T, ds_s[0:total]) * FACTOR
        for h in range(REP):
            cols = slice(h * HEAD_SIZE, (h + 1) * HEAD_SIZE)
            dq_ref[:, cols] = dqt[:, cols].T.astype(jnp.bfloat16)

    for n in range(LINKS + 1):
        pl.when(live == n)(functools.partial(work, n))

    @pl.when(b == block_count - 1)
    def _():
        near_ref[...] = near_acc[...]
        far_ref[...] = far_acc[...].astype(jnp.bfloat16)


def group_grads(chunk, links, header_blocks, index, queries, out_grad, extended, table, dq_prev):
    rows = queries.shape[0]
    block_count = rows // BLK
    groups = KEY_VALUE_HEADS // CHUNKS
    base = chunk * groups
    near_rows = extended.shape[0]
    far_rows = table.shape[0]
    wide = REP * HEAD_SIZE
    spec = lambda shape, f: pl.BlockSpec(shape, f)
    in_specs = [
        spec((BLK, wide), lambda g, b, *_: (b, base + g)),
        spec((BLK, wide), lambda g, b, *_: (b, base + g)),
        spec((near_rows, HEAD_SIZE), lambda g, b, *_: (0, base + g)),
        spec((near_rows, HEAD_SIZE), lambda g, b, *_: (0, KEY_VALUE_HEADS + base + g)),
        spec((far_rows, HEAD_SIZE), lambda g, b, *_: (0, g)),
        spec((far_rows, HEAD_SIZE), lambda g, b, *_: (0, groups + g)),
        pl.BlockSpec(memory_space=pl.ANY),
    ]
    args = [queries, out_grad, extended, extended, table, table]
    kernel = functools.partial(grad_kernel, block_count)
    aliases = {}
    if dq_prev is None:
        in_specs.pop()
        inner = kernel
        kernel = lambda *r: inner(*r[:9], None, *r[9:])
    else:
        args.append(dq_prev)
        aliases = {9: 0}
    span = (3 + LINKS) * BLK
    return pl.pallas_call(
        kernel,
        grid_spec=pltpu.PrefetchScalarGridSpec(
            num_scalar_prefetch=3,
            grid=(groups, block_count),
            in_specs=in_specs,
            out_specs=[
                spec((BLK, wide), lambda g, b, *_: (b, base + g)),
                spec((near_rows, 2 * HEAD_SIZE), lambda g, b, *_: (0, g)),
                spec((far_rows, 2 * HEAD_SIZE), lambda g, b, *_: (0, g)),
            ],
            scratch_shapes=[
                pltpu.VMEM((span, HEAD_SIZE), jnp.bfloat16),
                pltpu.VMEM((span, HEAD_SIZE), jnp.bfloat16),
                pltpu.VMEM((span, wide), jnp.bfloat16),
                pltpu.VMEM((span, wide), jnp.bfloat16),
                pltpu.VMEM((near_rows, 2 * HEAD_SIZE), jnp.float32),
                pltpu.VMEM((far_rows, 2 * HEAD_SIZE), jnp.float32),
            ],
        ),
        out_shape=[
            jax.ShapeDtypeStruct((rows, QUERY_HEADS * HEAD_SIZE), jnp.bfloat16),
            jax.ShapeDtypeStruct((near_rows, groups * 2 * HEAD_SIZE), jnp.float32),
            jax.ShapeDtypeStruct((far_rows, groups * 2 * HEAD_SIZE), jnp.bfloat16),
        ],
        input_output_aliases=aliases,
        compiler_params=pltpu.CompilerParams(dimension_semantics=("arbitrary", "arbitrary")),
        cost_estimate=pl.CostEstimate(flops=16_000_000_000 // CHUNKS, bytes_accessed=16_000_000 // CHUNKS,
                                      transcendentals=13_000_000 // CHUNKS),
        name="link_grads",
    )(links, header_blocks, index, *args)


def body(queries, keys, values, out_grad, links, header_blocks):
    rows = queries.shape[0]
    block_count = rows // BLK
    half = keys.shape[1]
    me = lax.axis_index("ctx")
    index = me.astype(jnp.int32).reshape(1)
    kv = jnp.concatenate([keys, values], axis=1)
    is_mine = header_blocks // block_count == me
    offset = jnp.sum(jnp.where(is_mine, header_blocks % block_count, 0)).astype(jnp.int32)
    holds = jnp.any(is_mine)
    slot = lax.dynamic_slice_in_dim(kv, offset * BLK, BLK, 0)
    width = half // CHUNKS
    tables = [
        lax.all_gather(
            jnp.concatenate([slot[:, c * width:(c + 1) * width], slot[:, half + c * width:half + (c + 1) * width]], axis=1),
            "ctx", axis=0, tiled=True)
        for c in range(CHUNKS)
    ]
    extended = jnp.concatenate([shifted(kv[rows - WIN:], "ctx", 1), kv], axis=0)
    peers = tables[0].shape[0] // BLK
    dq, key_parts, value_parts = None, [], []
    for c in range(CHUNKS):
        dq, near, far = group_grads(c, links, header_blocks, index, queries, out_grad, extended, tables[c], dq)
        back = shifted(near[:WIN].astype(jnp.bfloat16), "ctx", -1)
        own = lax.psum_scatter(far, "ctx", scatter_dimension=0, tiled=True)
        mask = (jnp.arange(block_count) == offset) & holds
        own = jnp.where(mask[:, None, None], own.astype(jnp.float32)[None], 0.0).reshape(rows, -1)
        local = near[WIN:] + own + jnp.pad(back.astype(jnp.float32), ((rows - WIN, 0), (0, 0)))
        local = local.reshape(rows, -1, 2, HEAD_SIZE)
        key_parts.append(local[:, :, 0].reshape(rows, -1))
        value_parts.append(local[:, :, 1].reshape(rows, -1))
    return dq, jnp.concatenate(key_parts, axis=1), jnp.concatenate(value_parts, axis=1)


def solution(mesh):
    row = P(("groups", "ctx"), None)
    return jax.shard_map(body, mesh=mesh, in_specs=(row, row, row, row, row, P("groups")),
                         out_specs=(row, row, row), check_vma=False)
```

time: 731 us -> 255 us (0.35)
  matrix products: 392 us -> 0 us
  local copies, waits for them, and re-layouts: 115 us -> 12.7 us
  Pallas kernels: 0 us -> 40 us
  other arithmetic: 47.7 us -> 12.6 us
  waiting for transfers between devices: 146 us -> 169 us
  loops' own time: 11.1 us -> 0 us
    dot_general x17 -> x0, matrix products: 346 us -> none  [the longest x4 147 us: block_grads(): jnp.einsum('gqrk,kgd->qgrd', d_scores, key_three_axes, preferred_element_...]
    sub x4 -> x0, matrix products: 45.2 us -> none  [block_grads(): weights = jnp.exp(scores - row_max)]
    pallas_call x0 -> x2, Pallas kernels: none -> 40 us  [group_grads(): pl.pallas_call(kernel, grid_spec=pltpu.PrefetchScalarGridSpec(num_scalar_...]
    dynamic_slice x28 -> x0, local copies, waits for them, and re-layouts: 37.4 us -> none  [the longest x8 17.7 us: one_block(): gradient_row_block = lax.dynamic_slice_in_dim(out_grad, row_start, BLK, 0)]
    dynamic_update_slice x16 -> x0, local copies, waits for them, and re-layouts: 32.9 us -> none  [the longest x8 23.1 us: one_block(): lax.dynamic_update_slice_in_dim(near_acc, current + key_value_gradient[:w...]
    scatter-add x5 -> x0, other arithmetic: 17.7 us -> none  [the longest x4 16.5 us: one_block(): far_acc = far_acc.at[holder].add(far_grad)]
    gather x8 -> x0, local copies, waits for them, and re-layouts: 13.8 us -> none  [the longest x4 11.2 us: one_block(): fetched = header_table[holder].reshape(LINKS * BLK, kv_width)]
    all_gather x1 -> x2, waiting for transfers between devices: 48 us -> 61.6 us  [body(): lax.all_gather(jnp.concatenate([slot[:, c * width:(c + 1) * width], slot[...]
  transfers between devices with their start and end apart: 4 -> 7, of which waited for: 4 -> 5; matrix products, arithmetic and copies ran while one was open for 1% -> 3% of each run, Pallas kernels for 0% -> 16%
where the time goes in v1:
time: 255 us; the launch traced here: 254 us
  waiting for transfers between devices  169 us (66%)
  Pallas kernels  40 us (16%)
  between operations  14.6 us (6%)
  local copies, waits for them, and re-layouts  12.7 us (5%)
  other arithmetic  12.6 us (5%)
  starting transfers between devices  5.18 us (2%)
    reduce_scatter x2, waiting for transfers between devices, body(): own = lax.psum_scatter(far, 'ctx', scatter_dimension=0, tiled=True)  106 us
    all_gather x2, waiting for transfers between devices, body(): lax.all_gather(jnp.concatenate([slot[:, c * width:(c + 1) * width], slot[...  61.6 us
    pallas_call x2, Pallas kernels, group_grads(): pl.pallas_call(kernel, grid_spec=pltpu.PrefetchScalarGridSpec(num_scalar_...  40 us
    slice x1, local copies, waits for them, and re-layouts, body(): value_parts.append(local[:, :, 1].reshape(rows, -1))  6.65 us
  transfers between devices with their start and end apart: 7, of which 5 were waited for; matrix products, arithmetic and copies ran while one was open for 3% of the time, Pallas kernels for 16%

profile of v1, /device:TPU:0, one launch (start us, length us, event | category | flops | bytes accessed | tf_op | source)
XLA Modules:
  0.0 254.0 jit_solution(16643318038170449215)
XLA Ops:
  7.2 1.3 compare_reduce_fusion
  8.5 1.4 fusion.4
  10.6 1.1 constant_dynamic-update-slice_fusion.1
  11.7 1.1 constant_dynamic-update-slice_fusion
  14.4 2.4 collective-permute-start
  16.8 1.5 collective-permute-done
  18.3 1.3 pad_maximum_fusion.r_5_.r_6_.k_ref.v_ref
  19.6 38.7 %all-gather.5.cloned.1.call-done.r_7_.r_8_ = bf16[2048,512]{1,0:T(8,128)(2,1)} async-done(((bf16[128,512]{1,0:T(8,128)(2,1)}), bf16[2048,512]{1,0:T(8,128)(2,1)}) %all-gather.5.cloned.1.call-update) | async-done | bytes 2097168 | tf_op jit(solution)/shard_map/all_gather | solution.py:199
  58.3 19.9 %link_grads.2 = (bf16[512,3584]{1,0:T(8,128)(2,1)}, f32[768,512]{1,0:T(8,128)}, bf16[2048,512]{1,0:T(8,128)(2,1)}) custom-call(s32[4,4]{1,0:T(4,128)} %links.1, s32[4]{0:T(128)} %headers.1, s32[1]{0:T(128)} %bitcast.r_2_.index, bf16[512,3584]{1,0:T(8,128)(2,1)} %q_ref.1, bf16[512,3584]{1,0:T(8,128)(2,1)} %o_ref.1, ...), custom_call_target="tpu_custom_call" | custom-call | flops 8000000000 | bytes 8000000 | tf_op jit(solution)/shard_map/link_grads/pallas_call | solution.py:153
  78.3 23.0 %all-gather.3.cloned.1.call-done.hk_ref.hv_ref = bf16[2048,512]{1,0:T(8,128)(2,1)} async-done(((bf16[128,512]{1,0:T(8,128)(2,1)}), bf16[2048,512]{1,0:T(8,128)(2,1)}) %all-gather.3.cloned.1.call-update) | async-done | bytes 2097168 | tf_op jit(solution)/shard_map/all_gather | solution.py:199
  101.2 20.1 %link_grads.3 = (bf16[512,3584]{1,0:T(8,128)(2,1)}, f32[768,512]{1,0:T(8,128)}, bf16[2048,512]{1,0:T(8,128)(2,1)}) custom-call(s32[4,4]{1,0:T(4,128)} %links.1, s32[4]{0:T(128)} %headers.1, s32[1]{0:T(128)} %bitcast.r_2_.index, bf16[512,3584]{1,0:T(8,128)(2,1)} %q_ref.1, bf16[512,3584]{1,0:T(8,128)(2,1)} %o_ref.1, ...), custom_call_target="tpu_custom_call", output_to_operand_aliasing={{0}: (9, {})} | custom-call | flops 8000000000 | bytes 8000000 | tf_op jit(solution)/shard_map/link_grads/pallas_call | solution.py:153
  121.4 1.1 slice.69
  122.5 1.1 slice.70
  123.6 1.3 collective-permute-start.1
  124.9 1.3 collective-permute-start.2
  126.2 1.3 compare_and_fusion
  127.5 42.3 %reduce-scatter.3.cloned.1.call-done = bf16[128,512]{1,0:T(8,128)(2,1)} async-done(((bf16[2048,512]{1,0:T(8,128)(2,1)}), bf16[128,512]{1,0:T(8,128)(2,1)}) %reduce-scatter.3.cloned.1.call-update) | async-done | bytes 131088 | tf_op jit(solution)/shard_map/reduce_scatter | solution.py:210
  169.8 0.9 convert_element_type.7
  170.7 63.4 %reduce-scatter.5.cloned.1.call-done = bf16[128,512]{1,0:T(8,128)(2,1)} async-done(((bf16[2048,512]{1,0:T(8,128)(2,1)}), bf16[128,512]{1,0:T(8,128)(2,1)}) %reduce-scatter.5.cloned.1.call-update) | async-done | bytes 131088 | tf_op jit(solution)/shard_map/reduce_scatter | solution.py:210
  234.1 0.9 convert_element_type.14
  235.1 1.9 fusion.3
  238.4 6.7 %slice_reduce_fusion = (f32[512,2,128]{2,1,0:T(2,128)S(1)}, f32[512,2,128]{2,1,0:T(2,128)S(1)}, f32[512,2,128]{2,1,0:T(2,128)S(1)}, f32[512,2,128]{2,1,0:T(2,128)S(1)}) fusion(f32[512,2,2,128]{3,2,1,0:T(2,128)S(1)} %reshape.30, f32[512,2,2,128]{3,2,1,0:T(2,128)S(1)} %reshape.29), kind=kLoop, calls=%fused_computation.13 | loop fusion | bytes 4194304 | tf_op jit(solution)/shard_map/slice | solution.py:216
  245.2 1.1 pad_maximum_fusion.1
  246.3 1.1 pad_maximum_fusion.2
  (21 shorter events, 3.2 us)
Async XLA Ops:
  7.2 51.1 %all-gather.5.cloned.1.call-start = ((), (), s32[]{:S(2)}) async-start(), calls=%async_computation.3 | async-start | bytes 2228224 | tf_op jit(solution)/shard_map/all_gather | solution.py:199
  13.6 87.7 %all-gather.3.cloned.1.call-start = ((), (), s32[]{:S(2)}) async-start(), calls=%async_computation.2 | async-start | bytes 2228224 | tf_op jit(solution)/shard_map/all_gather | solution.py:199
  14.3 155.5 %reduce-scatter.3.cloned.1.call-start = ((), (), s32[]{:S(2)}) async-start(), calls=%async_computation.4 | async-start | bytes 2228224 | tf_op jit(solution)/shard_map/reduce_scatter | solution.py:210
  14.4 3.9 %collective-permute-start = (bf16[256,1024]{1,0:T(8,128)(2,1)S(1)}, bf16[256,1024]{1,0:T(8,128)(2,1)S(1)}, u32[]{:S(2)}, u32[]{:S(2)}) collective-permute-start(bf16[256,1024]{1,0:T(8,128)(2,1)S(1)} %slice.54), channel_id=1, source_target_pairs={{0,1},{1,2},{2,3},{3,4},{4,5},{5,6},{6,7},{7,8},{8,9},{9,10},{10,1... | collective-permute-start | bytes 1572872 | tf_op jit(solution)/shard_map/ppermute | solution.py:27
  78.2 155.9 %reduce-scatter.5.cloned.1.call-start = ((), (), s32[]{:S(2)}) async-start(), calls=%async_computation.5 | async-start | bytes 2228224 | tf_op jit(solution)/shard_map/reduce_scatter | solution.py:210
  123.6 111.5 %collective-permute-start.1 = (bf16[256,512]{1,0:T(8,128)(2,1)S(1)}, bf16[256,512]{1,0:T(8,128)(2,1)S(1)}, u32[]{:S(2)}, u32[]{:S(2)}) collective-permute-start(bf16[256,512]{1,0:T(8,128)(2,1)S(1)} %slice.70), channel_id=1, source_target_pairs={{1,0},{2,1},{3,2},{4,3},{5,4},{6,5},{7,6},{8,7},{9,8},{10,9},{11,1... | collective-permute-start | bytes 786440 | tf_op jit(solution)/shard_map/ppermute | solution.py:27
  124.9 110.2 %collective-permute-start.2 = (bf16[256,512]{1,0:T(8,128)(2,1)S(1)}, bf16[256,512]{1,0:T(8,128)(2,1)S(1)}, u32[]{:S(2)}, u32[]{:S(2)}) collective-permute-start(bf16[256,512]{1,0:T(8,128)(2,1)S(1)} %slice.69), channel_id=1, source_target_pairs={{1,0},{2,1},{3,2},{4,3},{5,4},{6,5},{7,6},{8,7},{9,8},{10,9},{11,1... | collective-permute-start | bytes 786440 | tf_op jit(solution)/shard_map/ppermute | solution.py:27
Sparse Core Ops, SparseCore 0:
  13.7 44.5 all-gather.4
  61.0 40.1 all-gather.2
  105.0 64.7 reduce-scatter.2
  173.4 60.6 reduce-scatter.4
